TPU v7x, 512 devices: a whole 4x8x8 slice. The times are simulated.
512 devices in a mesh: depth: 16 (over y_hi, z), illum: 32 (over x, y_lo, core).
Axes of the slice: x: 4, y: 8 (y_hi: 2, y_lo: 4; y = y_hi * 4 + y_lo), z: 8, core: 2. Of those that a mesh axis runs over, the one named last changes fastest.
Arguments:
- amplitude: float32 [16, 256, 256], P('depth', 'illum'), may hold values from 0.92 to 1
- phase: float32 [16, 256, 256], P('depth', 'illum'), may hold values from -3.140625 to 3.140625
- kernel_phase: float32 [256, 256], replicated, may hold values from -3.140625 to 3.140625
- entry_field: float32 [2, 16, 32, 256, 256], P(None, 'depth', 'illum'), may hold values from -6 to 6
- cotangent: float32 [2, 32, 256, 256], P(None, 'illum'), may hold values from -6 to 6
Outputs:
- slice_grad: float32 [2, 16, 256, 256], P(None, 'depth', 'illum')
All inputs are finite; a program needn't handle non-finite values.
Results may differ from a plain program's by a relative error of at most 0.0003.
Values sent between devices are 32-bit elements; how exact they have to be, the bound alone decides.
No kernel may reach another device: no remote copies, remote signals or barrier semaphores. Data moves between devices by JAX's collectives and lax.ppermute only.
A program may use at most 64 MiB of HBM per device.

v0:
```python
import functools
import math

import jax
import jax.numpy as jnp
import numpy as np
from jax import lax
from jax.experimental import pallas as pl
from jax.experimental.pallas import tpu as pltpu
from jax.sharding import Mesh, PartitionSpec as P

AXES = ("yh", "z", "x", "yl", "c")
SIZES = (2, 8, 4, 4, 2)
N = 256
HALF = 128
SLICES = 16
COLOURS = 4
PEERS = 64
CHUNKS = ((1, SLICES),)
F32 = jnp.float32
BF16 = jnp.bfloat16


def _real_form(angle):
    c, s = np.cos(angle), np.sin(angle)
    return np.block([[c, -s], [s, c]])


def _split_np(m):
    hi = m.astype(BF16)
    return hi, (m - hi.astype(np.float64)).astype(BF16)


@functools.cache
def tables():
    n = np.arange(HALF)
    even = _real_form(2 * np.pi * ((n[:, None] * n[None, :]) % HALF) / HALF)
    odd = _real_form(2 * np.pi * ((n[:, None] * (2 * n[None, :] + 1)) % N) / N)
    core, x, yl, r = np.meshgrid(np.arange(2), np.arange(2), np.arange(4), np.arange(8), indexing="ij")
    order = (x * 64 + yl * 16 + core * 8 + r).reshape(-1)
    both = np.concatenate([order, order + HALF])
    right, left = [], []
    for m in (even, odd, even.T, odd.T):
        hi, lo = _split_np(m)
        right.append(np.stack([hi, lo]))
    for m in (even.T[:, both], odd.T[:, both], even[both, :], odd[both, :]):
        hi, lo = _split_np(m)
        left.append(np.stack([hi, lo]))
    return np.stack(right), np.stack(left)


def sincos(angle):
    turns = jnp.round(angle * (2.0 / math.pi))
    r = ((angle - turns * 1.5703125) - turns * 4.837512969970703125e-4) - turns * 7.54978995489188216e-8
    quadrant = turns.astype(jnp.int32)
    z = r * r
    sine = r + r * z * (-1.6666654611e-1 + z * (8.3321608736e-3 - z * 1.9515295891e-4))
    cosine = 1.0 - 0.5 * z + z * z * (4.166664568298827e-2 + z * (-1.388731625493765e-3 + z * 2.443315711809948e-5))
    odd = (quadrant & 1) == 1
    s, c = jnp.where(odd, cosine, sine), jnp.where(odd, sine, cosine)
    s = jnp.where((quadrant & 2) == 2, -s, s)
    c = jnp.where(((quadrant + 1) & 2) == 2, -c, c)
    return s, c


def prepare_kernel(amp_ref, phase_ref, out_ref):
    amp = amp_ref[0]
    sine, cosine = sincos(phase_ref[0])
    re, im = amp * cosine, amp * sine
    for q, tile in enumerate((re[:, :HALF], re[:, HALF:], im[:, :HALF], im[:, HALF:])):
        for chip in range(PEERS):
            out_ref[chip, q] = tile


def prepare(amplitude, phase):
    return pl.pallas_call(
        prepare_kernel,
        out_shape=pltpu.VMEM((PEERS, 4, 8, HALF), F32),
        name="prepare",
    )(amplitude, phase)


def split(value):
    hi = value.astype(BF16)
    return hi, (value - hi.astype(F32)).astype(BF16)


def dot_right(value, table):
    hi, lo = split(value)
    wide = jnp.concatenate([table[0], table[0], table[1]], axis=0)
    return jnp.dot(jnp.concatenate([hi, lo, hi], axis=1), wide, preferred_element_type=F32)


def dot_left(table, value):
    hi, lo = split(value)
    wide = jnp.concatenate([table[0], table[0], table[1]], axis=1)
    return jnp.dot(wide, jnp.concatenate([hi, lo, hi], axis=0), preferred_element_type=F32)


def propagate(chi_l, chi_r, right_ref, left_ref, kc_ref, ks_ref):
    ye = dot_right(chi_l + chi_r, right_ref[0])
    yo = dot_right(chi_l - chi_r, right_ref[1])
    re = jnp.concatenate([ye[:, :HALF], yo[:, :HALF]], axis=1)
    im = jnp.concatenate([ye[:, HALF:], yo[:, HALF:]], axis=1)

    def first(v):
        return jnp.concatenate([v[0:64], v[128:192]], axis=0)

    def second(v):
        return jnp.concatenate([v[64:128], v[192:256]], axis=0)

    a = jnp.concatenate([first(re), first(im)], axis=0)
    b = jnp.concatenate([second(re), second(im)], axis=0)
    freqs = [dot_left(left_ref[i], mixed) for i, mixed in enumerate((a + b, a - b))]
    out = []
    for i, freq in enumerate(freqs):
        fr, fi = freq[:HALF], freq[HALF:]
        c, s = kc_ref[i], ks_ref[i]
        weighted = jnp.concatenate([fr * c + fi * s, fi * c - fr * s], axis=0)
        out.append(dot_left(left_ref[2 + i], weighted))
    top, low = out[0] + out[1], out[0] - out[1]

    def rows(part):
        t, l = top[part * HALF : (part + 1) * HALF], low[part * HALF : (part + 1) * HALF]
        return jnp.concatenate([t[:64], l[:64], t[64:], l[64:]], axis=0)

    re, im = rows(0), rows(1)
    ue = dot_right(jnp.concatenate([re[:, :HALF], im[:, :HALF]], axis=1), right_ref[2])
    uo = dot_right(jnp.concatenate([re[:, HALF:], im[:, HALF:]], axis=1), right_ref[3])
    return ue + uo, ue - uo


def three(value):
    hi = value.astype(BF16)
    rest = value - hi.astype(F32)
    mid = rest.astype(BF16)
    return hi, mid, (rest - mid.astype(F32)).astype(BF16)


def held(ref, part, half):
    lanes = slice(half * HALF, (half + 1) * HALF)
    return jnp.concatenate([ref[part, :, c, :, lanes].reshape(HALF, HALF) for c in range(2)], axis=0)


def begin_kernel(order_ref, cot_ref, kern_ref, right_ref, left_ref, u_ref, kc_ref, ks_ref):
    del order_ref
    row = lax.broadcasted_iota(jnp.int32, (N, N), 0)
    col = lax.broadcasted_iota(jnp.int32, (N, N), 1)
    picks = jnp.where(col == jnp.where(row < HALF, 2 * row, 2 * row - (N - 1)), 1.0, 0.0).astype(BF16)
    picks_t = jnp.where(row == jnp.where(col < HALF, 2 * col, 2 * col - (N - 1)), 1.0, 0.0).astype(BF16)
    angle = kern_ref[...]
    angle = sum(jnp.dot(picks, p, preferred_element_type=F32) for p in three(angle))
    angle = sum(jnp.dot(p, picks_t, preferred_element_type=F32) for p in three(angle))
    scale = 1.0 / (N * N)
    sine, cosine = sincos(angle)
    kc_ref[...] = (cosine * scale).reshape(2, HALF, N)
    ks_ref[...] = (sine * scale).reshape(2, HALF, N)
    fields = (jnp.concatenate([held(cot_ref, 0, h), held(cot_ref, 1, h)], axis=1) for h in range(2))
    u_ref[0], u_ref[1] = propagate(*fields, right_ref, left_ref, kc_ref, ks_ref)


def chain_kernel(where_ref, u_ref, kc_ref, ks_ref, right_ref, left_ref, psi_hbm, *rest):
    gathered, (own_ref, send_ref, t_ref, chi_ref, psi_ref, sem, psi_sem) = rest[:8], rest[8:]
    depth, colour, core = where_ref[0], where_ref[1], where_ref[2]
    other = 1 - core
    near = lax.rem(colour + jnp.where(core == 0, 3, 1), 4)
    far = lax.rem(colour + jnp.where(core == 0, 1, 3), 4)
    across = lax.rem(colour + 2, 4)
    places = (
        (colour, core), (colour, other),
        (near, core), (across, core), (near, other),
        (far, other), (across, other), (far, core),
    )

    def copies(chunk):
        low, high = CHUNKS[chunk]
        span = slice(low, high)
        return [
            pltpu.make_async_copy(ref.at[span], t_ref.at[hue, rows, span], sem.at[chunk])
            for ref, (hue, rows) in zip(gathered, places)
        ]

    for chunk, (_, high) in enumerate(CHUNKS):

        @pl.when(depth < high - 1)
        def _():
            for copy in copies(chunk):
                copy.start()

    psi_copy = pltpu.make_async_copy(psi_hbm, psi_ref, psi_sem)
    psi_copy.start()
    chi_ref[...] = u_ref[...]

    def body(i, _):
        j = SLICES - 1 - i
        for chunk, (_, high) in enumerate(CHUNKS):

            @pl.when(j == high - 1)
            def _():
                for copy in copies(chunk):
                    copy.wait()

        hues = [(j + e) & 3 for e in range(COLOURS)]

        def rows_of(q):
            tiles = [
                t_ref[hues[(x + 2 * yl) & 3], c, j, yl, q] for c in range(2) for x in range(4) for yl in range(4)
            ]
            return jnp.concatenate(tiles, axis=0)

        chi = []
        for h in range(2):
            u = chi_ref[h]
            ur, ui = u[:, :HALF], u[:, HALF:]
            tr, ti = rows_of(h), rows_of(2 + h)
            chi.append(jnp.concatenate([ur * tr + ui * ti, ui * tr - ur * ti], axis=1))
        chi_ref[0], chi_ref[1] = propagate(*chi, right_ref, left_ref, kc_ref, ks_ref)
        return 0

    lax.fori_loop(0, SLICES - 1 - depth, body, 0)

    psi_copy.wait()
    for h in range(2):
        lanes = slice(h * HALF, (h + 1) * HALF)
        u = chi_ref[h]
        ur, ui = u[:, :HALF], u[:, HALF:]
        pr, pi = held(psi_ref, 0, h), held(psi_ref, 1, h)
        for part, g in enumerate((ur * pr + ui * pi, ui * pr - ur * pi)):
            first, second = g[:HALF], g[HALF:]
            own_ref[:, part, :, lanes] = jnp.where(core == 0, first, second).reshape(16, 8, HALF)
            send_ref[:, part, :, lanes] = jnp.where(core == 0, second, first).reshape(16, 8, HALF)


VMEM = pl.BlockSpec(memory_space=pltpu.VMEM)
SMEM = pl.BlockSpec(memory_space=pltpu.SMEM)
ANY = pl.BlockSpec(memory_space=pl.ANY)


def begin(order, cotangent, kernel_phase):
    right, left = tables()
    field = jax.ShapeDtypeStruct((2, N, N), F32)
    table = jax.ShapeDtypeStruct((2, HALF, N), F32)
    return pl.pallas_call(
        begin_kernel,
        out_shape=(field, table, table),
        in_specs=[SMEM] + [VMEM] * 4,
        out_specs=(VMEM,) * 3,
        compiler_params=pltpu.CompilerParams(vmem_limit_bytes=24 << 20),
        cost_estimate=pl.CostEstimate(flops=2_000_000_000, bytes_accessed=4 << 20, transcendentals=1 << 17),
        name="begin",
    )(order, cotangent.reshape(2, 16, 2, 8, N), kernel_phase, jnp.asarray(right), jnp.asarray(left))


def chain(where, begun, psi, gathered):
    right, left = tables()
    part = jax.ShapeDtypeStruct((16, 2, 8, N), F32)
    return pl.pallas_call(
        chain_kernel,
        out_shape=(part, part),
        in_specs=[SMEM] + [VMEM] * 5 + [ANY] * 9,
        out_specs=(VMEM, VMEM),
        scratch_shapes=[
            pltpu.VMEM((COLOURS, 2, SLICES, 4, 4, 8, HALF), F32),
            pltpu.VMEM((2, N, N), F32),
            pltpu.VMEM((2, 16, 2, 8, N), F32),
            pltpu.SemaphoreType.DMA((len(CHUNKS),)),
            pltpu.SemaphoreType.DMA,
        ],
        compiler_params=pltpu.CompilerParams(vmem_limit_bytes=22 << 20),
        name="chain",
    )(where, *begun, jnp.asarray(right), jnp.asarray(left), psi.reshape(2, 16, 2, 8, N), *gathered)


def send(value, target):
    pairs = []
    for source in range(int(np.prod(SIZES))):
        yh, z, x, yl, c = (int(v) for v in np.unravel_index(source, SIZES))
        y, z, x, c = target(yh * 4 + yl, z, x, c)
        y %= 8
        pairs.append((source, int(np.ravel_multi_index((y // 4, z % 8, x % 4, y % 4, c), SIZES))))
    return lax.ppermute(value, AXES, pairs)


def colour_groups():
    groups = {}
    for yh, z, yl, x, c in np.ndindex(2, 8, 4, 4, 2):
        device = int(np.ravel_multi_index((yh, z, x, yl, c), SIZES))
        groups.setdefault(((x + 2 * yl + z) % COLOURS, c), []).append(device)
    return [groups[key] for key in sorted(groups)]


def per_device(amplitude, phase, kernel_phase, entry_field, cotangent):
    yh, z, x, yl, c = (lax.axis_index(a) for a in AXES)
    where = jnp.stack([yh * 8 + z, lax.rem(x + 2 * yl + z, 4), c]).astype(jnp.int32)
    own = lax.all_to_all(prepare(amplitude, phase), AXES, 0, 0, axis_index_groups=colour_groups())
    own = own.reshape(SLICES, 4, 4, 8, HALF)
    sign = (1, -1)

    def partner(v):
        return send(v, lambda y, z, x, c: (y, z, x, 1 - c))

    from_x = send(own, lambda y, z, x, c: (y, z, x + sign[c], c))
    from_y = send(own, lambda y, z, x, c: (y + sign[c], z, x, c))
    from_z = send(own, lambda y, z, x, c: (y, z + sign[1 - c], x, 1 - c))
    theirs = partner(own)
    order, _ = lax.optimization_barrier((where, own[:1, :1, :1]))
    begun = begin(order, cotangent.reshape(2, N, N), kernel_phase)
    from_x, begun = lax.optimization_barrier((from_x, begun))
    their_x = partner(from_x)
    their_y = partner(from_y)
    their_z = partner(from_z)
    gathered = (own, theirs, from_x, from_y, from_z, their_x, their_y, their_z)
    mine, others = chain(where, begun, entry_field.reshape(2, N, N), gathered)
    parts = lax.all_to_all(mine + partner(others), ("x", "yl"), 0, 0)
    return (jnp.sum(parts, axis=0) * (1.0 / math.sqrt(32)))[:, None]


def solution(mesh):
    fine = Mesh(mesh.devices.reshape(SIZES), AXES)
    depth, illum = ("yh", "z"), ("x", "yl", "c")
    return jax.shard_map(
        per_device,
        mesh=fine,
        in_specs=(
            P(depth, illum, None),
            P(depth, illum, None),
            P(),
            P(None, depth, illum, None, None),
            P(None, illum, None, None),
        ),
        out_specs=P(None, depth, illum, None),
        check_vma=False,
    )
```

profile of v0, /device:TPU:1, one launch (start us, length us, event | category | flops | bytes accessed | tf_op | source)
XLA Modules:
  0.0 127.4 jit_solution(6387110087320314818)
XLA Ops:
  0.0 0.8 prepare.1
  0.9 0.0 copy-start
  0.9 0.0 copy-start.4
  0.9 49.4 %all_to_all.10 = f32[64,4,8,128]{3,2,1,0:T(8,128)S(1)} all-to-all(f32[64,4,8,128]{3,2,1,0:T(8,128)S(1)} %prepare.1), channel_id=1, replica_groups={{0,18,4,22,56,42,60,46,80,66,84,70,104,122,108,126,128,146,132,150,184,..., dimensions={0} | all-to-all | bytes 2097152 | tf_op jit(solution)/shard_map/all_to_all | solution.py:295
  50.2 2.9 %collective-permute-start = (f32[16,4,4,8,128]{4,3,2,1,0:T(8,128)S(1)}, f32[16,4,4,8,128]{4,3,2,1,0:T(8,128)}, u32[]{:S(2)}, u32[]{:S(2)}) collective-permute-start(f32[16,4,4,8,128]{4,3,2,1,0:T(8,128)S(1)} %bitcast.8), channel_id=1, source_target_pairs={{0,8},{1,25},{2,10},{3,27},{4,12},{5,29},{6,14},{7,31},{8,16},{9,1... | collective-permute-start | bytes 3145736 | tf_op jit(solution)/shard_map/ppermute | solution.py:281
  53.2 5.1 %collective-permute-start.3 = (f32[16,4,4,8,128]{4,3,2,1,0:T(8,128)S(1)}, f32[16,4,4,8,128]{4,3,2,1,0:T(8,128)}, u32[]{:S(2)}, u32[]{:S(2)}) collective-permute-start(f32[16,4,4,8,128]{4,3,2,1,0:T(8,128)S(1)} %bitcast.9), channel_id=1, source_target_pairs={{0,225},{1,32},{2,227},{3,34},{4,229},{5,36},{6,231},{7,38},{8,233... | collective-permute-start | bytes 3145736 | tf_op jit(solution)/shard_map/ppermute | solution.py:281
  58.3 3.0 %collective-permute-start.2 = (f32[16,4,4,8,128]{4,3,2,1,0:T(8,128)S(1)}, f32[16,4,4,8,128]{4,3,2,1,0:T(8,128)}, u32[]{:S(2)}, u32[]{:S(2)}) collective-permute-start(f32[16,4,4,8,128]{4,3,2,1,0:T(8,128)S(1)} %bitcast.10), channel_id=1, source_target_pairs={{0,2},{1,263},{2,4},{3,1},{4,6},{5,3},{6,256},{7,5},{8,10},{9,271}... | collective-permute-start | bytes 3145736 | tf_op jit(solution)/shard_map/ppermute | solution.py:281
  61.3 0.1 pad_add_fusion.order_ref.where_ref
  61.4 0.0 copy-done
  61.4 0.0 copy-done.4
  61.4 0.0 copy-start.1
  61.4 1.2 copy-done.1
  62.6 0.0 copy-start.3
  62.6 1.0 copy-done.3
  63.7 0.0 copy-start.2
  63.7 2.8 %begin.1 = (f32[2,256,256]{2,1,0:T(8,128)S(1)}, f32[2,128,256]{2,1,0:T(8,128)S(1)}, f32[2,128,256]{2,1,0:T(8,128)S(1)}) custom-call(s32[3]{0:T(128)S(1)} %pad_add_fusion.order_ref.where_ref, f32[2,16,2,8,256]{4,3,2,1,0:T(8,128)S(1)} %bitcast.14, f32[256,256]{1,0:T(8,128)S(1)} %copy-done.4, bf16[4,2,256,256]{3,2,1,0:T(8,128)(2,1)S(1)} %copy-done.1, ...), custom_call_target="tpu_custom_call" | custom-call | flops 2000000000 | bytes 4194304 | tf_op jit(solution)/shard_map/begin/pallas_call | solution.py:243
  66.5 1.9 %collective-permute-start.1 = (f32[16,4,4,8,128]{4,3,2,1,0:T(8,128)S(1)}, f32[16,4,4,8,128]{4,3,2,1,0:T(8,128)S(1)}, u32[]{:S(2)}, u32[]{:S(2)}) collective-permute-start(f32[16,4,4,8,128]{4,3,2,1,0:T(8,128)S(1)} %bitcast.11), channel_id=1, source_target_pairs={{0,1},{1,0},{2,3},{3,2},{4,5},{5,4},{6,7},{7,6},{8,9},{9,8},{10,11... | collective-permute-start | bytes 3145736 | tf_op jit(solution)/shard_map/ppermute | solution.py:281
  68.4 0.0 collective-permute-done.rest_2_
  68.4 2.8 %collective-permute-done.3.rest_4_ = f32[16,4,4,8,128]{4,3,2,1,0:T(8,128)} collective-permute-done((f32[16,4,4,8,128]{4,3,2,1,0:T(8,128)S(1)}, f32[16,4,4,8,128]{4,3,2,1,0:T(8,128)}, u32[]{:S(2)}, u32[]{:S(2)}) %collective-permute-start.3) | collective-permute-done | bytes 1048608 | tf_op jit(solution)/shard_map/ppermute | solution.py:281
  71.2 2.0 %collective-permute-start.6 = (f32[16,4,4,8,128]{4,3,2,1,0:T(8,128)}, f32[16,4,4,8,128]{4,3,2,1,0:T(8,128)S(1)}, u32[]{:S(2)}, u32[]{:S(2)}) collective-permute-start(f32[16,4,4,8,128]{4,3,2,1,0:T(8,128)} %collective-permute-done.3.rest_4_), channel_id=1, source_target_pairs={{0,1},{1,0},{2,3},{3,2},{4,5},{5,4},{6,7},{7,6},{8,9},{9,8},{10,11... | collective-permute-start | bytes 3145736 | tf_op jit(solution)/shard_map/ppermute | solution.py:281
  73.2 0.8 collective-permute-done.2.rest_3_
  74.0 1.9 %collective-permute-start.5 = (f32[16,4,4,8,128]{4,3,2,1,0:T(8,128)}, f32[16,4,4,8,128]{4,3,2,1,0:T(8,128)S(1)}, u32[]{:S(2)}, u32[]{:S(2)}) collective-permute-start(f32[16,4,4,8,128]{4,3,2,1,0:T(8,128)} %collective-permute-done.2.rest_3_), channel_id=1, source_target_pairs={{0,1},{1,0},{2,3},{3,2},{4,5},{5,4},{6,7},{7,6},{8,9},{9,8},{10,11... | collective-permute-start | bytes 3145736 | tf_op jit(solution)/shard_map/ppermute | solution.py:281
  75.9 2.4 %collective-permute-start.4 = (f32[16,4,4,8,128]{4,3,2,1,0:T(8,128)}, f32[16,4,4,8,128]{4,3,2,1,0:T(8,128)S(1)}, u32[]{:S(2)}, u32[]{:S(2)}) collective-permute-start(f32[16,4,4,8,128]{4,3,2,1,0:T(8,128)} %collective-permute-done.rest_2_), channel_id=1, source_target_pairs={{0,1},{1,0},{2,3},{3,2},{4,5},{5,4},{6,7},{7,6},{8,9},{9,8},{10,11... | collective-permute-start | bytes 3145736 | tf_op jit(solution)/shard_map/ppermute | solution.py:281
  78.3 0.0 collective-permute-done.1.rest_1_
  78.3 0.0 collective-permute-done.6.rest_7_
  78.3 0.4 collective-permute-done.5.rest_6_
  78.7 2.1 %collective-permute-done.4.rest_5_ = f32[16,4,4,8,128]{4,3,2,1,0:T(8,128)S(1)} collective-permute-done((f32[16,4,4,8,128]{4,3,2,1,0:T(8,128)}, f32[16,4,4,8,128]{4,3,2,1,0:T(8,128)S(1)}, u32[]{:S(2)}, u32[]{:S(2)}) %collective-permute-start.4) | collective-permute-done | bytes 1048608 | tf_op jit(solution)/shard_map/ppermute | solution.py:281
  80.8 0.0 copy-done.2
  80.8 25.8 %chain.1 = (f32[16,2,8,256]{3,2,1,0:T(8,128)S(1)}, f32[16,2,8,256]{3,2,1,0:T(8,128)S(1)}) custom-call(s32[3]{0:T(128)S(1)} %pad_add_fusion.order_ref.where_ref, f32[2,256,256]{2,1,0:T(8,128)S(1)} %get-tuple-element.17.u_ref, f32[2,128,256]{2,1,0:T(8,128)S(1)} %get-tuple-element.18.kc_ref, f32[2,128,256]{2,1,0:T(8,128)S(1)} %get-tuple-element.19.ks_ref, ...), custom_call_target="tpu_custom_call" | custom-call | tf_op jit(solution)/shard_map/chain/pallas_call | solution.py:257
  106.5 2.3 %collective-permute-start.7 = (f32[16,2,8,256]{3,2,1,0:T(8,128)S(1)}, f32[16,2,8,256]{3,2,1,0:T(8,128)S(1)}, u32[]{:S(2)}, u32[]{:S(2)}) collective-permute-start(f32[16,2,8,256]{3,2,1,0:T(8,128)S(1)} %get-tuple-element.22), channel_id=1, source_target_pairs={{0,1},{1,0},{2,3},{3,2},{4,5},{5,4},{6,7},{7,6},{8,9},{9,8},{10,11... | collective-permute-start | bytes 786440 | tf_op jit(solution)/shard_map/ppermute | solution.py:281
  108.8 1.1 collective-permute-done.7
  110.0 16.7 %all_to_all.11 = f32[16,2,8,256]{3,2,1,0:T(8,128)S(1)} all-to-all(f32[16,2,8,256]{3,2,1,0:T(8,128)S(1)} %add.15), channel_id=1, replica_groups=mesh['yh'=2,'z'=8,'x'=4,'yl'=4,'c'=2] {'x','yl'}, dimensions={0} | all-to-all | bytes 524288 | tf_op jit(solution)/shard_map/all_to_all | solution.py:314
  126.8 0.6 multiply_bitcast_fusion
  (2 shorter events, 0.1 us)
Async XLA Ops:
  0.9 60.5 %copy-start = (bf16[4,2,256,256]{3,2,1,0:T(8,128)(2,1)S(1)}, bf16[4,2,256,256]{3,2,1,0:T(8,128)(2,1)}, u32[]{:S(2)}) copy-start(bf16[4,2,256,256]{3,2,1,0:T(8,128)(2,1)} %constant.38.clone.left_ref) | copy-start | bytes 3145732
  0.9 60.5 %copy-start.4 = (f32[256,256]{1,0:T(8,128)S(1)}, f32[256,256]{1,0:T(8,128)}, u32[]{:S(2)}) copy-start(f32[256,256]{1,0:T(8,128)} %kern_ref.1) | copy-start | bytes 786436
  50.2 18.1 %collective-permute-start = (f32[16,4,4,8,128]{4,3,2,1,0:T(8,128)S(1)}, f32[16,4,4,8,128]{4,3,2,1,0:T(8,128)}, u32[]{:S(2)}, u32[]{:S(2)}) collective-permute-start(f32[16,4,4,8,128]{4,3,2,1,0:T(8,128)S(1)} %bitcast.8), channel_id=1, source_target_pairs={{0,8},{1,25},{2,10},{3,27},{4,12},{5,29},{6,14},{7,31},{8,16},{9,1... | collective-permute-start | bytes 3145736 | tf_op jit(solution)/shard_map/ppermute | solution.py:281
  53.2 18.0 %collective-permute-start.3 = (f32[16,4,4,8,128]{4,3,2,1,0:T(8,128)S(1)}, f32[16,4,4,8,128]{4,3,2,1,0:T(8,128)}, u32[]{:S(2)}, u32[]{:S(2)}) collective-permute-start(f32[16,4,4,8,128]{4,3,2,1,0:T(8,128)S(1)} %bitcast.9), channel_id=1, source_target_pairs={{0,225},{1,32},{2,227},{3,34},{4,229},{5,36},{6,231},{7,38},{8,233... | collective-permute-start | bytes 3145736 | tf_op jit(solution)/shard_map/ppermute | solution.py:281
  58.3 15.6 %collective-permute-start.2 = (f32[16,4,4,8,128]{4,3,2,1,0:T(8,128)S(1)}, f32[16,4,4,8,128]{4,3,2,1,0:T(8,128)}, u32[]{:S(2)}, u32[]{:S(2)}) collective-permute-start(f32[16,4,4,8,128]{4,3,2,1,0:T(8,128)S(1)} %bitcast.10), channel_id=1, source_target_pairs={{0,2},{1,263},{2,4},{3,1},{4,6},{5,3},{6,256},{7,5},{8,10},{9,271}... | collective-permute-start | bytes 3145736 | tf_op jit(solution)/shard_map/ppermute | solution.py:281
  61.4 1.2 copy-start.1
  62.6 1.0 copy-start.3
  63.7 17.1 %copy-start.2 = (f32[2,1,1,256,256]{4,3,2,1,0:T(8,128)S(1)}, f32[2,1,1,256,256]{4,3,2,1,0:T(8,128)}, u32[]{:S(2)}) copy-start(f32[2,1,1,256,256]{4,3,2,1,0:T(8,128)} %param.10) | copy-start | bytes 1572868
  66.5 11.8 %collective-permute-start.1 = (f32[16,4,4,8,128]{4,3,2,1,0:T(8,128)S(1)}, f32[16,4,4,8,128]{4,3,2,1,0:T(8,128)S(1)}, u32[]{:S(2)}, u32[]{:S(2)}) collective-permute-start(f32[16,4,4,8,128]{4,3,2,1,0:T(8,128)S(1)} %bitcast.11), channel_id=1, source_target_pairs={{0,1},{1,0},{2,3},{3,2},{4,5},{5,4},{6,7},{7,6},{8,9},{9,8},{10,11... | collective-permute-start | bytes 3145736 | tf_op jit(solution)/shard_map/ppermute | solution.py:281
  71.2 7.1 %collective-permute-start.6 = (f32[16,4,4,8,128]{4,3,2,1,0:T(8,128)}, f32[16,4,4,8,128]{4,3,2,1,0:T(8,128)S(1)}, u32[]{:S(2)}, u32[]{:S(2)}) collective-permute-start(f32[16,4,4,8,128]{4,3,2,1,0:T(8,128)} %collective-permute-done.3.rest_4_), channel_id=1, source_target_pairs={{0,1},{1,0},{2,3},{3,2},{4,5},{5,4},{6,7},{7,6},{8,9},{9,8},{10,11... | collective-permute-start | bytes 3145736 | tf_op jit(solution)/shard_map/ppermute | solution.py:281
  74.0 4.8 %collective-permute-start.5 = (f32[16,4,4,8,128]{4,3,2,1,0:T(8,128)}, f32[16,4,4,8,128]{4,3,2,1,0:T(8,128)S(1)}, u32[]{:S(2)}, u32[]{:S(2)}) collective-permute-start(f32[16,4,4,8,128]{4,3,2,1,0:T(8,128)} %collective-permute-done.2.rest_3_), channel_id=1, source_target_pairs={{0,1},{1,0},{2,3},{3,2},{4,5},{5,4},{6,7},{7,6},{8,9},{9,8},{10,11... | collective-permute-start | bytes 3145736 | tf_op jit(solution)/shard_map/ppermute | solution.py:281
  75.9 4.9 %collective-permute-start.4 = (f32[16,4,4,8,128]{4,3,2,1,0:T(8,128)}, f32[16,4,4,8,128]{4,3,2,1,0:T(8,128)S(1)}, u32[]{:S(2)}, u32[]{:S(2)}) collective-permute-start(f32[16,4,4,8,128]{4,3,2,1,0:T(8,128)} %collective-permute-done.rest_2_), channel_id=1, source_target_pairs={{0,1},{1,0},{2,3},{3,2},{4,5},{5,4},{6,7},{7,6},{8,9},{9,8},{10,11... | collective-permute-start | bytes 3145736 | tf_op jit(solution)/shard_map/ppermute | solution.py:281
  106.5 3.4 %collective-permute-start.7 = (f32[16,2,8,256]{3,2,1,0:T(8,128)S(1)}, f32[16,2,8,256]{3,2,1,0:T(8,128)S(1)}, u32[]{:S(2)}, u32[]{:S(2)}) collective-permute-start(f32[16,2,8,256]{3,2,1,0:T(8,128)S(1)} %get-tuple-element.22), channel_id=1, source_target_pairs={{0,1},{1,0},{2,3},{3,2},{4,5},{5,4},{6,7},{7,6},{8,9},{9,8},{10,11... | collective-permute-start | bytes 786440 | tf_op jit(solution)/shard_map/ppermute | solution.py:281
where the time goes:
time: 128 us; the launch traced here: 127 us
  blocking collectives  66.1 us (52%)
  Pallas kernels  29.4 us (23%)
  starting transfers between devices  21.6 us (17%)
  waiting for transfers between devices  7.14 us (6%)
  local copies, waits for them, and re-layouts  2.28 us (2%)
    all_to_all x1, blocking collectives, per_device(): lax.all_to_all(prepare(amplitude, phase), AXES, 0, 0, axis_index_groups=c...  49.4 us
    pallas_call x1, Pallas kernels, chain(): pl.pallas_call(chain_kernel, out_shape=(part, part), in_specs=[SMEM] + [V...  25.8 us
    ppermute x8, starting transfers between devices, send(): return lax.ppermute(value, AXES, pairs)  21.6 us
    all_to_all x1, blocking collectives, per_device(): parts = lax.all_to_all(mine + partner(others), ('x', 'yl'), 0, 0)  16.7 us
    ppermute x8, waiting for transfers between devices, send(): return lax.ppermute(value, AXES, pairs)  7.14 us
    pallas_call x1, Pallas kernels, begin(): pl.pallas_call(begin_kernel, out_shape=(field, table, table), in_specs=[S...  2.78 us
  transfers between devices with their start and end apart: 8, of which 5 were waited for; matrix products, arithmetic and copies ran while one was open for 0% of the time, Pallas kernels for 2%

commit v1 on v0

--- a/solution.py
+++ b/solution.py
@@ -16,7 +16,7 @@
 SLICES = 16
 COLOURS = 4
 PEERS = 64
-CHUNKS = ((1, SLICES),)
+EARLY = 5
 F32 = jnp.float32
 BF16 = jnp.bfloat16
 
@@ -46,7 +46,7 @@
     for m in (even.T[:, both], odd.T[:, both], even[both, :], odd[both, :]):
         hi, lo = _split_np(m)
         left.append(np.stack([hi, lo]))
-    return np.stack(right), np.stack(left)
+    return np.stack(right + left)
 
 
 def sincos(angle):
@@ -97,9 +97,9 @@
     return jnp.dot(wide, jnp.concatenate([hi, lo, hi], axis=0), preferred_element_type=F32)
 
 
-def propagate(chi_l, chi_r, right_ref, left_ref, kc_ref, ks_ref):
-    ye = dot_right(chi_l + chi_r, right_ref[0])
-    yo = dot_right(chi_l - chi_r, right_ref[1])
+def propagate(chi_l, chi_r, table_ref, kc_ref, ks_ref):
+    ye = dot_right(chi_l + chi_r, table_ref[0])
+    yo = dot_right(chi_l - chi_r, table_ref[1])
     re = jnp.concatenate([ye[:, :HALF], yo[:, :HALF]], axis=1)
     im = jnp.concatenate([ye[:, HALF:], yo[:, HALF:]], axis=1)
 
@@ -111,13 +111,13 @@
 
     a = jnp.concatenate([first(re), first(im)], axis=0)
     b = jnp.concatenate([second(re), second(im)], axis=0)
-    freqs = [dot_left(left_ref[i], mixed) for i, mixed in enumerate((a + b, a - b))]
+    freqs = [dot_left(table_ref[4 + i], mixed) for i, mixed in enumerate((a + b, a - b))]
     out = []
     for i, freq in enumerate(freqs):
         fr, fi = freq[:HALF], freq[HALF:]
         c, s = kc_ref[i], ks_ref[i]
         weighted = jnp.concatenate([fr * c + fi * s, fi * c - fr * s], axis=0)
-        out.append(dot_left(left_ref[2 + i], weighted))
+        out.append(dot_left(table_ref[6 + i], weighted))
     top, low = out[0] + out[1], out[0] - out[1]
 
     def rows(part):
@@ -125,8 +125,8 @@
         return jnp.concatenate([t[:64], l[:64], t[64:], l[64:]], axis=0)
 
     re, im = rows(0), rows(1)
-    ue = dot_right(jnp.concatenate([re[:, :HALF], im[:, :HALF]], axis=1), right_ref[2])
-    uo = dot_right(jnp.concatenate([re[:, HALF:], im[:, HALF:]], axis=1), right_ref[3])
+    ue = dot_right(jnp.concatenate([re[:, :HALF], im[:, :HALF]], axis=1), table_ref[2])
+    uo = dot_right(jnp.concatenate([re[:, HALF:], im[:, HALF:]], axis=1), table_ref[3])
     return ue + uo, ue - uo
 
 
@@ -142,7 +142,7 @@
     return jnp.concatenate([ref[part, :, c, :, lanes].reshape(HALF, HALF) for c in range(2)], axis=0)
 
 
-def begin_kernel(order_ref, cot_ref, kern_ref, right_ref, left_ref, u_ref, kc_ref, ks_ref):
+def begin_kernel(order_ref, cot_ref, kern_ref, table_ref, u_ref, kc_ref, ks_ref):
     del order_ref
     row = lax.broadcasted_iota(jnp.int32, (N, N), 0)
     col = lax.broadcasted_iota(jnp.int32, (N, N), 1)
@@ -156,50 +156,54 @@
     kc_ref[...] = (cosine * scale).reshape(2, HALF, N)
     ks_ref[...] = (sine * scale).reshape(2, HALF, N)
     fields = (jnp.concatenate([held(cot_ref, 0, h), held(cot_ref, 1, h)], axis=1) for h in range(2))
-    u_ref[0], u_ref[1] = propagate(*fields, right_ref, left_ref, kc_ref, ks_ref)
-
-
-def chain_kernel(where_ref, u_ref, kc_ref, ks_ref, right_ref, left_ref, psi_hbm, *rest):
-    gathered, (own_ref, send_ref, t_ref, chi_ref, psi_ref, sem, psi_sem) = rest[:8], rest[8:]
-    depth, colour, core = where_ref[0], where_ref[1], where_ref[2]
+    u_ref[0], u_ref[1] = propagate(*fields, table_ref, kc_ref, ks_ref)
+
+
+def places(where_ref):
+    colour, core = where_ref[1], where_ref[2]
     other = 1 - core
-    near = lax.rem(colour + jnp.where(core == 0, 3, 1), 4)
-    far = lax.rem(colour + jnp.where(core == 0, 1, 3), 4)
-    across = lax.rem(colour + 2, 4)
-    places = (
+    near = lax.rem(colour + jnp.where(core == 0, 3, 1), COLOURS)
+    far = lax.rem(colour + jnp.where(core == 0, 1, 3), COLOURS)
+    across = lax.rem(colour + 2, COLOURS)
+    return (
         (colour, core), (colour, other),
         (near, core), (across, core), (near, other),
         (far, other), (across, other), (far, core),
     )
 
-    def copies(chunk):
-        low, high = CHUNKS[chunk]
-        span = slice(low, high)
-        return [
-            pltpu.make_async_copy(ref.at[span], t_ref.at[hue, rows, span], sem.at[chunk])
-            for ref, (hue, rows) in zip(gathered, places)
-        ]
-
-    for chunk, (_, high) in enumerate(CHUNKS):
-
-        @pl.when(depth < high - 1)
-        def _():
-            for copy in copies(chunk):
-                copy.start()
-
+
+def placing(arrays, slots, t_ref, sem):
+    used = slice(1, SLICES)
+    return [
+        pltpu.make_async_copy(ref.at[used], t_ref.at[hue, rows, used], sem)
+        for ref, (hue, rows) in zip(arrays, slots)
+    ]
+
+
+def place_kernel(where_ref, *rest):
+    arrays, (t_ref, sem) = rest[:EARLY], rest[EARLY:]
+    copies = placing(arrays, places(where_ref)[:EARLY], t_ref, sem)
+    for copy in copies:
+        copy.start()
+    for copy in copies:
+        copy.wait()
+
+
+def chain_kernel(where_ref, u_ref, kc_ref, ks_ref, table_ref, psi_hbm, placed_ref, *rest):
+    del placed_ref
+    late, (own_ref, send_ref, t_ref, chi_ref, psi_ref, sem, psi_sem) = rest[: 8 - EARLY], rest[8 - EARLY :]
+    depth, core = where_ref[0], where_ref[2]
+    copies = placing(late, places(where_ref)[EARLY:], t_ref, sem)
+    for copy in copies:
+        copy.start()
     psi_copy = pltpu.make_async_copy(psi_hbm, psi_ref, psi_sem)
     psi_copy.start()
     chi_ref[...] = u_ref[...]
+    for copy in copies:
+        copy.wait()
 
     def body(i, _):
         j = SLICES - 1 - i
-        for chunk, (_, high) in enumerate(CHUNKS):
-
-            @pl.when(j == high - 1)
-            def _():
-                for copy in copies(chunk):
-                    copy.wait()
-
         hues = [(j + e) & 3 for e in range(COLOURS)]
 
         def rows_of(q):
@@ -214,7 +218,7 @@
             ur, ui = u[:, :HALF], u[:, HALF:]
             tr, ti = rows_of(h), rows_of(2 + h)
             chi.append(jnp.concatenate([ur * tr + ui * ti, ui * tr - ur * ti], axis=1))
-        chi_ref[0], chi_ref[1] = propagate(*chi, right_ref, left_ref, kc_ref, ks_ref)
+        chi_ref[0], chi_ref[1] = propagate(*chi, table_ref, kc_ref, ks_ref)
         return 0
 
     lax.fori_loop(0, SLICES - 1 - depth, body, 0)
@@ -237,38 +241,53 @@
 
 
 def begin(order, cotangent, kernel_phase):
-    right, left = tables()
     field = jax.ShapeDtypeStruct((2, N, N), F32)
     table = jax.ShapeDtypeStruct((2, HALF, N), F32)
     return pl.pallas_call(
         begin_kernel,
         out_shape=(field, table, table),
-        in_specs=[SMEM] + [VMEM] * 4,
+        in_specs=[SMEM] + [VMEM] * 3,
         out_specs=(VMEM,) * 3,
-        compiler_params=pltpu.CompilerParams(vmem_limit_bytes=24 << 20),
+        compiler_params=pltpu.CompilerParams(vmem_limit_bytes=10 << 20),
         cost_estimate=pl.CostEstimate(flops=2_000_000_000, bytes_accessed=4 << 20, transcendentals=1 << 17),
         name="begin",
-    )(order, cotangent.reshape(2, 16, 2, 8, N), kernel_phase, jnp.asarray(right), jnp.asarray(left))
-
-
-def chain(where, begun, psi, gathered):
-    right, left = tables()
+    )(order, cotangent.reshape(2, 16, 2, 8, N), kernel_phase, jnp.asarray(tables()))
+
+
+PLACED = (COLOURS, 2, SLICES, 4, 4, 8, HALF)
+
+
+def place(where, arrays):
+    return pl.pallas_call(
+        place_kernel,
+        out_shape=pltpu.VMEM(PLACED, F32),
+        in_specs=[SMEM] + [ANY] * EARLY,
+        out_specs=VMEM,
+        scratch_shapes=[pltpu.SemaphoreType.DMA],
+        compiler_params=pltpu.CompilerParams(vmem_limit_bytes=2 << 20),
+        cost_estimate=pl.CostEstimate(flops=0, bytes_accessed=10 << 20, transcendentals=0),
+        name="place",
+    )(where, *arrays)
+
+
+def chain(where, begun, psi, placed, late):
     part = jax.ShapeDtypeStruct((16, 2, 8, N), F32)
-    return pl.pallas_call(
+    own, send_, _ = pl.pallas_call(
         chain_kernel,
-        out_shape=(part, part),
-        in_specs=[SMEM] + [VMEM] * 5 + [ANY] * 9,
-        out_specs=(VMEM, VMEM),
+        out_shape=(part, part, pltpu.VMEM(PLACED, F32)),
+        in_specs=[SMEM] + [VMEM] * 4 + [ANY, VMEM] + [ANY] * (8 - EARLY),
+        out_specs=(VMEM,) * 3,
+        input_output_aliases={6: 2},
         scratch_shapes=[
-            pltpu.VMEM((COLOURS, 2, SLICES, 4, 4, 8, HALF), F32),
             pltpu.VMEM((2, N, N), F32),
             pltpu.VMEM((2, 16, 2, 8, N), F32),
-            pltpu.SemaphoreType.DMA((len(CHUNKS),)),
+            pltpu.SemaphoreType.DMA,
             pltpu.SemaphoreType.DMA,
         ],
-        compiler_params=pltpu.CompilerParams(vmem_limit_bytes=22 << 20),
+        compiler_params=pltpu.CompilerParams(vmem_limit_bytes=10 << 20),
         name="chain",
-    )(where, *begun, jnp.asarray(right), jnp.asarray(left), psi.reshape(2, 16, 2, 8, N), *gathered)
+    )(where, *begun, jnp.asarray(tables()), psi.reshape(2, 16, 2, 8, N), placed, *late)
+    return own, send_
 
 
 def send(value, target):
@@ -293,6 +312,8 @@
     yh, z, x, yl, c = (lax.axis_index(a) for a in AXES)
     where = jnp.stack([yh * 8 + z, lax.rem(x + 2 * yl + z, 4), c]).astype(jnp.int32)
     own = lax.all_to_all(prepare(amplitude, phase), AXES, 0, 0, axis_index_groups=colour_groups())
+    begun = begin(where, cotangent.reshape(2, N, N), kernel_phase)
+    own, begun = lax.optimization_barrier((own, begun))
     own = own.reshape(SLICES, 4, 4, 8, HALF)
     sign = (1, -1)
 
@@ -303,14 +324,12 @@
     from_y = send(own, lambda y, z, x, c: (y + sign[c], z, x, c))
     from_z = send(own, lambda y, z, x, c: (y, z + sign[1 - c], x, 1 - c))
     theirs = partner(own)
-    order, _ = lax.optimization_barrier((where, own[:1, :1, :1]))
-    begun = begin(order, cotangent.reshape(2, N, N), kernel_phase)
-    from_x, begun = lax.optimization_barrier((from_x, begun))
     their_x = partner(from_x)
     their_y = partner(from_y)
     their_z = partner(from_z)
-    gathered = (own, theirs, from_x, from_y, from_z, their_x, their_y, their_z)
-    mine, others = chain(where, begun, entry_field.reshape(2, N, N), gathered)
+    placed = place(where, (own, theirs, from_x, from_y, from_z))
+    psi = entry_field.reshape(2, N, N)
+    mine, others = chain(where, begun, psi, placed, (their_x, their_y, their_z))
     parts = lax.all_to_all(mine + partner(others), ("x", "yl"), 0, 0)
     return (jnp.sum(parts, axis=0) * (1.0 / math.sqrt(32)))[:, None]
 

time: 128 us -> 123 us (0.961)
  blocking collectives: 66.1 us -> 13.3 us
  starting transfers between devices: 21.6 us -> 43.5 us
  waiting for transfers between devices: 7.14 us -> 28.9 us
  local copies, waits for them, and re-layouts: 2.28 us -> 5.1 us
  Pallas kernels: 29.4 us -> 30.9 us
    all_to_all x1 -> x0, blocking collectives: 49.4 us -> none  [per_device(): lax.all_to_all(prepare(amplitude, phase), AXES, 0, 0, axis_index_groups=c...]
    all_to_all x0 -> x1, waiting for transfers between devices: none -> 21.9 us  [per_device(): lax.all_to_all(prepare(amplitude, phase), AXES, 0, 0, axis_index_groups=c...]
    all_to_all x0 -> x1, starting transfers between devices: none -> 19.6 us  [per_device(): lax.all_to_all(prepare(amplitude, phase), AXES, 0, 0, axis_index_groups=c...]
    all_to_all x1, blocking collectives: 16.7 us -> 13.3 us  [per_device(): parts = lax.all_to_all(mine + partner(others), ('x', 'yl'), 0, 0)]
    unnamed x10 -> x18, local copies, waits for them, and re-layouts: 2.28 us -> 5.1 us
    ppermute x8, starting transfers between devices: 21.6 us -> 24 us  [send(): return lax.ppermute(value, AXES, pairs)]
    pallas_call x1 -> x2, Pallas kernels: 25.8 us -> 26.3 us  [the longest x1 24.2 us: chain(): pl.pallas_call(chain_kernel, out_shape=(part, part, pltpu.VMEM(PLACED, F3...]
  transfers between devices with their start and end apart: 8 -> 9, of which waited for: 5 -> 6; matrix products, arithmetic and copies ran while one was open for 0% -> 0% of each run, Pallas kernels for 2% -> 4%
where the time goes in v1:
time: 123 us
  starting transfers between devices  43.5 us (35%)
  Pallas kernels  30.9 us (25%)
  waiting for transfers between devices  28.9 us (23%)
  blocking collectives  13.3 us (11%)
  local copies, waits for them, and re-layouts  5.1 us (4%)
    pallas_call x1, Pallas kernels, chain(): pl.pallas_call(chain_kernel, out_shape=(part, part, pltpu.VMEM(PLACED, F3...  24.2 us
    ppermute x8, starting transfers between devices, send(): return lax.ppermute(value, AXES, pairs)  24 us
    all_to_all x1, waiting for transfers between devices, per_device(): lax.all_to_all(prepare(amplitude, phase), AXES, 0, 0, axis_index_groups=c...  21.9 us
    all_to_all x1, starting transfers between devices, per_device(): lax.all_to_all(prepare(amplitude, phase), AXES, 0, 0, axis_index_groups=c...  19.6 us
    all_to_all x1, blocking collectives, per_device(): parts = lax.all_to_all(mine + partner(others), ('x', 'yl'), 0, 0)  13.3 us
    ppermute x8, waiting for transfers between devices, send(): return lax.ppermute(value, AXES, pairs)  7.06 us
    unnamed x18, local copies, waits for them, and re-layouts  5.1 us
    pallas_call x1, Pallas kernels, begin(): pl.pallas_call(begin_kernel, out_shape=(field, table, table), in_specs=[S...  2.79 us
  transfers between devices with their start and end apart: 9, of which 6 were waited for; matrix products, arithmetic and copies ran while one was open for 0% of the time, Pallas kernels for 4%

profile of v1, /device:TPU:1, one launch (start us, length us, event | category | flops | bytes accessed | tf_op | source)
XLA Modules:
  0.0 122.7 jit_solution(8866401551499510176)
XLA Ops:
  0.0 1.8 %prepare.1 = f32[64,4,8,128]{3,2,1,0:T(8,128)} custom-call(f32[1,8,256]{2,1,0:T(8,128)} %amp_ref.1, f32[1,8,256]{2,1,0:T(8,128)} %phase_ref.1), custom_call_target="tpu_custom_call" | custom-call | tf_op jit(solution)/shard_map/prepare/pallas_call | solution.py:76
  1.8 19.6 %all-to-all-start = ((f32[64,4,8,128]{3,2,1,0:T(8,128)}), f32[64,4,8,128]{3,2,1,0:T(8,128)S(1)}, u32[]{:S(2)}, u32[]{:S(2)}) async-start(f32[64,4,8,128]{3,2,1,0:T(8,128)} %prepare.1), calls=%async_computation | async-start | bytes 2097152 | tf_op jit(solution)/shard_map/all_to_all | solution.py:314
  21.4 0.1 pad_add_fusion.order_ref.where_ref
  21.5 0.0 copy-start
  21.5 1.6 %copy-done = bf16[8,2,256,256]{3,2,1,0:T(8,128)(2,1)S(1)} copy-done((bf16[8,2,256,256]{3,2,1,0:T(8,128)(2,1)S(1)}, bf16[8,2,256,256]{3,2,1,0:T(8,128)(2,1)}, u32[]{:S(2)}) %copy-start) | copy-done | bytes 2097176
  23.1 0.0 copy-start.7
  23.1 1.0 copy-done.7
  24.1 0.0 copy-start.8
  24.1 0.9 copy-done.8
  25.1 2.8 %begin.1 = (f32[2,256,256]{2,1,0:T(8,128)S(1)}, f32[2,128,256]{2,1,0:T(8,128)S(1)}, f32[2,128,256]{2,1,0:T(8,128)S(1)}) custom-call(s32[3]{0:T(128)S(1)} %pad_add_fusion.order_ref.where_ref, f32[2,16,2,8,256]{4,3,2,1,0:T(8,128)S(1)} %bitcast.14, f32[256,256]{1,0:T(8,128)S(1)} %copy-done.8, bf16[8,2,256,256]{3,2,1,0:T(8,128)(2,1)S(1)} %copy-done), custom_call_target="tpu_custom_call" | custom-call | flops 2000000000 | bytes 4194304 | tf_op jit(solution)/shard_map/begin/pallas_call | solution.py:246
  27.9 0.0 copy-start.3
  27.9 0.8 copy-done.3
  28.7 0.0 copy-start.5
  28.7 0.7 copy-done.5
  29.4 0.0 copy-start.1
  29.4 21.9 %all-to-all-done = f32[64,4,8,128]{3,2,1,0:T(8,128)S(1)} async-done(((f32[64,4,8,128]{3,2,1,0:T(8,128)}), f32[64,4,8,128]{3,2,1,0:T(8,128)S(1)}, u32[]{:S(2)}, u32[]{:S(2)}) %all-to-all-start) | async-done | bytes 1048608 | tf_op jit(solution)/shard_map/all_to_all | solution.py:314
  51.3 0.0 copy-start.2
  51.3 0.0 copy-start.4
  51.3 0.0 copy-start.6
  51.3 5.6 %collective-permute-start.3 = (f32[16,4,4,8,128]{4,3,2,1,0:T(8,128)S(1)}, f32[16,4,4,8,128]{4,3,2,1,0:T(8,128)S(1)}, u32[]{:S(2)}, u32[]{:S(2)}) collective-permute-start(f32[16,4,4,8,128]{4,3,2,1,0:T(8,128)S(1)} %bitcast.8), channel_id=1, source_target_pairs={{0,225},{1,32},{2,227},{3,34},{4,229},{5,36},{6,231},{7,38},{8,233... | collective-permute-start | bytes 3145736 | tf_op jit(solution)/shard_map/ppermute | solution.py:300
  56.8 1.9 %collective-permute-start.2 = (f32[16,4,4,8,128]{4,3,2,1,0:T(8,128)S(1)}, f32[16,4,4,8,128]{4,3,2,1,0:T(8,128)S(1)}, u32[]{:S(2)}, u32[]{:S(2)}) collective-permute-start(f32[16,4,4,8,128]{4,3,2,1,0:T(8,128)S(1)} %bitcast.9), channel_id=1, source_target_pairs={{0,2},{1,263},{2,4},{3,1},{4,6},{5,3},{6,256},{7,5},{8,10},{9,271}... | collective-permute-start | bytes 3145736 | tf_op jit(solution)/shard_map/ppermute | solution.py:300
  58.8 2.2 %collective-permute-start.1 = (f32[16,4,4,8,128]{4,3,2,1,0:T(8,128)S(1)}, f32[16,4,4,8,128]{4,3,2,1,0:T(8,128)S(1)}, u32[]{:S(2)}, u32[]{:S(2)}) collective-permute-start(f32[16,4,4,8,128]{4,3,2,1,0:T(8,128)S(1)} %bitcast.10), channel_id=1, source_target_pairs={{0,8},{1,25},{2,10},{3,27},{4,12},{5,29},{6,14},{7,31},{8,16},{9,1... | collective-permute-start | bytes 3145736 | tf_op jit(solution)/shard_map/ppermute | solution.py:300
  60.9 3.8 %collective-permute-start = (f32[16,4,4,8,128]{4,3,2,1,0:T(8,128)S(1)}, f32[16,4,4,8,128]{4,3,2,1,0:T(8,128)S(1)}, u32[]{:S(2)}, u32[]{:S(2)}) collective-permute-start(f32[16,4,4,8,128]{4,3,2,1,0:T(8,128)S(1)} %bitcast.11), channel_id=1, source_target_pairs={{0,1},{1,0},{2,3},{3,2},{4,5},{5,4},{6,7},{7,6},{8,9},{9,8},{10,11... | collective-permute-start | bytes 3145736 | tf_op jit(solution)/shard_map/ppermute | solution.py:300
  64.7 4.9 %collective-permute-done.3.rest_4_ = f32[16,4,4,8,128]{4,3,2,1,0:T(8,128)S(1)} collective-permute-done((f32[16,4,4,8,128]{4,3,2,1,0:T(8,128)S(1)}, f32[16,4,4,8,128]{4,3,2,1,0:T(8,128)S(1)}, u32[]{:S(2)}, u32[]{:S(2)}) %collective-permute-start.3) | collective-permute-done | bytes 1048608 | tf_op jit(solution)/shard_map/ppermute | solution.py:300
  69.6 2.2 %collective-permute-start.6 = (f32[16,4,4,8,128]{4,3,2,1,0:T(8,128)S(1)}, f32[16,4,4,8,128]{4,3,2,1,0:T(8,128)S(1)}, u32[]{:S(2)}, u32[]{:S(2)}) collective-permute-start(f32[16,4,4,8,128]{4,3,2,1,0:T(8,128)S(1)} %collective-permute-done.3.rest_4_), channel_id=1, source_target_pairs={{0,1},{1,0},{2,3},{3,2},{4,5},{5,4},{6,7},{7,6},{8,9},{9,8},{10,11... | collective-permute-start | bytes 3145736 | tf_op jit(solution)/shard_map/ppermute | solution.py:300
  71.9 0.8 collective-permute-done.2.rest_3_
  72.7 1.9 %collective-permute-start.5 = (f32[16,4,4,8,128]{4,3,2,1,0:T(8,128)S(1)}, f32[16,4,4,8,128]{4,3,2,1,0:T(8,128)S(1)}, u32[]{:S(2)}, u32[]{:S(2)}) collective-permute-start(f32[16,4,4,8,128]{4,3,2,1,0:T(8,128)S(1)} %collective-permute-done.2.rest_3_), channel_id=1, source_target_pairs={{0,1},{1,0},{2,3},{3,2},{4,5},{5,4},{6,7},{7,6},{8,9},{9,8},{10,11... | collective-permute-start | bytes 3145736 | tf_op jit(solution)/shard_map/ppermute | solution.py:300
  74.6 0.1 collective-permute-done.1.rest_2_
  74.7 4.1 %collective-permute-start.4 = (f32[16,4,4,8,128]{4,3,2,1,0:T(8,128)S(1)}, f32[16,4,4,8,128]{4,3,2,1,0:T(8,128)S(1)}, u32[]{:S(2)}, u32[]{:S(2)}) collective-permute-start(f32[16,4,4,8,128]{4,3,2,1,0:T(8,128)S(1)} %collective-permute-done.1.rest_2_), channel_id=1, source_target_pairs={{0,1},{1,0},{2,3},{3,2},{4,5},{5,4},{6,7},{7,6},{8,9},{9,8},{10,11... | collective-permute-start | bytes 3145736 | tf_op jit(solution)/shard_map/ppermute | solution.py:300
  78.8 0.0 collective-permute-done.rest_1_
  78.8 2.1 %place.1.placed_ref = f32[4,2,16,4,4,8,128]{6,5,4,3,2,1,0:T(8,128)S(1)} custom-call(s32[3]{0:T(128)S(1)} %pad_add_fusion.order_ref.where_ref, f32[16,4,4,8,128]{4,3,2,1,0:T(8,128)S(1)} %bitcast.12, f32[16,4,4,8,128]{4,3,2,1,0:T(8,128)S(1)} %collective-permute-done.rest_1_, f32[16,4,4,8,128]{4,3,2,1,0:T(8,128)S(1)} %collective-permute-done.1.rest_2_, ...), custom_call_target="tpu_custom_call" | custom-call | bytes 10485760 | tf_op jit(solution)/shard_map/place/pallas_call | solution.py:261
  80.9 0.0 collective-permute-done.6.rest_2_
  80.9 0.0 collective-permute-done.5.rest_1_
  80.9 0.1 collective-permute-done.4.rest_0_
  81.1 0.0 copy-done.1
  81.1 0.0 copy-done.2
  81.1 0.0 copy-done.4
  81.1 0.0 copy-done.6
  81.1 24.2 %chain.1 = (f32[16,2,8,256]{3,2,1,0:T(8,128)S(1)}, f32[16,2,8,256]{3,2,1,0:T(8,128)S(1)}, f32[4,2,16,4,4,8,128]{6,5,4,3,2,1,0:T(8,128)S(1)}) custom-call(s32[3]{0:T(128)S(1)} %pad_add_fusion.order_ref.where_ref, f32[2,256,256]{2,1,0:T(8,128)S(1)} %copy-done.4, f32[2,128,256]{2,1,0:T(8,128)S(1)} %get-tuple-element.18.kc_ref, ...), custom_call_target="tpu_custom_call", output_to_operand_aliasing={{2}: (6, {})} | custom-call | tf_op jit(solution)/shard_map/chain/pallas_call | solution.py:275
  105.3 2.3 %collective-permute-start.7 = (f32[16,2,8,256]{3,2,1,0:T(8,128)S(1)}, f32[16,2,8,256]{3,2,1,0:T(8,128)S(1)}, u32[]{:S(2)}, u32[]{:S(2)}) collective-permute-start(f32[16,2,8,256]{3,2,1,0:T(8,128)S(1)} %get-tuple-element.22), channel_id=1, source_target_pairs={{0,1},{1,0},{2,3},{3,2},{4,5},{5,4},{6,7},{7,6},{8,9},{9,8},{10,11... | collective-permute-start | bytes 786440 | tf_op jit(solution)/shard_map/ppermute | solution.py:300
  107.6 1.1 collective-permute-done.7
  108.7 13.3 %all_to_all.10 = f32[16,2,8,256]{3,2,1,0:T(8,128)S(1)} all-to-all(f32[16,2,8,256]{3,2,1,0:T(8,128)S(1)} %add.15), channel_id=1, replica_groups=mesh['yh'=2,'z'=8,'x'=4,'yl'=4,'c'=2] {'x','yl'}, dimensions={0} | all-to-all | bytes 524288 | tf_op jit(solution)/shard_map/all_to_all | solution.py:333
  122.1 0.6 multiply_bitcast_fusion
  (2 shorter events, 0.1 us)
Async XLA Ops:
  1.8 49.4 %all-to-all-start = ((f32[64,4,8,128]{3,2,1,0:T(8,128)}), f32[64,4,8,128]{3,2,1,0:T(8,128)S(1)}, u32[]{:S(2)}, u32[]{:S(2)}) async-start(f32[64,4,8,128]{3,2,1,0:T(8,128)} %prepare.1), calls=%async_computation | async-start | bytes 2097152 | tf_op jit(solution)/shard_map/all_to_all | solution.py:314
  21.5 1.6 %copy-start = (bf16[8,2,256,256]{3,2,1,0:T(8,128)(2,1)S(1)}, bf16[8,2,256,256]{3,2,1,0:T(8,128)(2,1)}, u32[]{:S(2)}) copy-start(bf16[8,2,256,256]{3,2,1,0:T(8,128)(2,1)} %constant.35.clone.table_ref) | copy-start | bytes 6291460
  23.1 1.0 copy-start.7
  24.1 0.9 copy-start.8
  27.9 0.8 copy-start.3
  28.7 0.7 copy-start.5
  29.4 51.7 %copy-start.1 = (bf16[8,2,256,256]{3,2,1,0:T(8,128)(2,1)S(1)}, bf16[8,2,256,256]{3,2,1,0:T(8,128)(2,1)}, u32[]{:S(2)}) copy-start(bf16[8,2,256,256]{3,2,1,0:T(8,128)(2,1)} %constant.35.clone.table_ref) | copy-start | bytes 6291460
  51.3 29.8 %copy-start.2 = (f32[2,1,1,256,256]{4,3,2,1,0:T(8,128)S(1)}, f32[2,1,1,256,256]{4,3,2,1,0:T(8,128)}, u32[]{:S(2)}) copy-start(f32[2,1,1,256,256]{4,3,2,1,0:T(8,128)} %param.9) | copy-start | bytes 1572868
  51.3 29.8 %copy-start.4 = (f32[2,256,256]{2,1,0:T(8,128)S(1)}, f32[2,256,256]{2,1,0:T(8,128)}, u32[]{:S(2)}) copy-start(f32[2,256,256]{2,1,0:T(8,128)} %copy-done.3) | copy-start | bytes 1572868
  51.3 29.8 %copy-start.6 = (f32[2,128,256]{2,1,0:T(8,128)S(1)}, f32[2,128,256]{2,1,0:T(8,128)}, u32[]{:S(2)}) copy-start(f32[2,128,256]{2,1,0:T(8,128)} %copy-done.5) | copy-start | bytes 786436
  51.3 18.3 %collective-permute-start.3 = (f32[16,4,4,8,128]{4,3,2,1,0:T(8,128)S(1)}, f32[16,4,4,8,128]{4,3,2,1,0:T(8,128)S(1)}, u32[]{:S(2)}, u32[]{:S(2)}) collective-permute-start(f32[16,4,4,8,128]{4,3,2,1,0:T(8,128)S(1)} %bitcast.8), channel_id=1, source_target_pairs={{0,225},{1,32},{2,227},{3,34},{4,229},{5,36},{6,231},{7,38},{8,233... | collective-permute-start | bytes 3145736 | tf_op jit(solution)/shard_map/ppermute | solution.py:300
  56.8 15.8 %collective-permute-start.2 = (f32[16,4,4,8,128]{4,3,2,1,0:T(8,128)S(1)}, f32[16,4,4,8,128]{4,3,2,1,0:T(8,128)S(1)}, u32[]{:S(2)}, u32[]{:S(2)}) collective-permute-start(f32[16,4,4,8,128]{4,3,2,1,0:T(8,128)S(1)} %bitcast.9), channel_id=1, source_target_pairs={{0,2},{1,263},{2,4},{3,1},{4,6},{5,3},{6,256},{7,5},{8,10},{9,271}... | collective-permute-start | bytes 3145736 | tf_op jit(solution)/shard_map/ppermute | solution.py:300
  58.8 15.9 %collective-permute-start.1 = (f32[16,4,4,8,128]{4,3,2,1,0:T(8,128)S(1)}, f32[16,4,4,8,128]{4,3,2,1,0:T(8,128)S(1)}, u32[]{:S(2)}, u32[]{:S(2)}) collective-permute-start(f32[16,4,4,8,128]{4,3,2,1,0:T(8,128)S(1)} %bitcast.10), channel_id=1, source_target_pairs={{0,8},{1,25},{2,10},{3,27},{4,12},{5,29},{6,14},{7,31},{8,16},{9,1... | collective-permute-start | bytes 3145736 | tf_op jit(solution)/shard_map/ppermute | solution.py:300
  60.9 17.9 %collective-permute-start = (f32[16,4,4,8,128]{4,3,2,1,0:T(8,128)S(1)}, f32[16,4,4,8,128]{4,3,2,1,0:T(8,128)S(1)}, u32[]{:S(2)}, u32[]{:S(2)}) collective-permute-start(f32[16,4,4,8,128]{4,3,2,1,0:T(8,128)S(1)} %bitcast.11), channel_id=1, source_target_pairs={{0,1},{1,0},{2,3},{3,2},{4,5},{5,4},{6,7},{7,6},{8,9},{9,8},{10,11... | collective-permute-start | bytes 3145736 | tf_op jit(solution)/shard_map/ppermute | solution.py:300
  69.6 11.3 %collective-permute-start.6 = (f32[16,4,4,8,128]{4,3,2,1,0:T(8,128)S(1)}, f32[16,4,4,8,128]{4,3,2,1,0:T(8,128)S(1)}, u32[]{:S(2)}, u32[]{:S(2)}) collective-permute-start(f32[16,4,4,8,128]{4,3,2,1,0:T(8,128)S(1)} %collective-permute-done.3.rest_4_), channel_id=1, source_target_pairs={{0,1},{1,0},{2,3},{3,2},{4,5},{5,4},{6,7},{7,6},{8,9},{9,8},{10,11... | collective-permute-start | bytes 3145736 | tf_op jit(solution)/shard_map/ppermute | solution.py:300
  72.7 8.3 %collective-permute-start.5 = (f32[16,4,4,8,128]{4,3,2,1,0:T(8,128)S(1)}, f32[16,4,4,8,128]{4,3,2,1,0:T(8,128)S(1)}, u32[]{:S(2)}, u32[]{:S(2)}) collective-permute-start(f32[16,4,4,8,128]{4,3,2,1,0:T(8,128)S(1)} %collective-permute-done.2.rest_3_), channel_id=1, source_target_pairs={{0,1},{1,0},{2,3},{3,2},{4,5},{5,4},{6,7},{7,6},{8,9},{9,8},{10,11... | collective-permute-start | bytes 3145736 | tf_op jit(solution)/shard_map/ppermute | solution.py:300
  74.7 6.4 %collective-permute-start.4 = (f32[16,4,4,8,128]{4,3,2,1,0:T(8,128)S(1)}, f32[16,4,4,8,128]{4,3,2,1,0:T(8,128)S(1)}, u32[]{:S(2)}, u32[]{:S(2)}) collective-permute-start(f32[16,4,4,8,128]{4,3,2,1,0:T(8,128)S(1)} %collective-permute-done.1.rest_2_), channel_id=1, source_target_pairs={{0,1},{1,0},{2,3},{3,2},{4,5},{5,4},{6,7},{7,6},{8,9},{9,8},{10,11... | collective-permute-start | bytes 3145736 | tf_op jit(solution)/shard_map/ppermute | solution.py:300
  105.3 3.4 %collective-permute-start.7 = (f32[16,2,8,256]{3,2,1,0:T(8,128)S(1)}, f32[16,2,8,256]{3,2,1,0:T(8,128)S(1)}, u32[]{:S(2)}, u32[]{:S(2)}) collective-permute-start(f32[16,2,8,256]{3,2,1,0:T(8,128)S(1)} %get-tuple-element.22), channel_id=1, source_target_pairs={{0,1},{1,0},{2,3},{3,2},{4,5},{5,4},{6,7},{7,6},{8,9},{9,8},{10,11... | collective-permute-start | bytes 786440 | tf_op jit(solution)/shard_map/ppermute | solution.py:300
